TPU v7x, 32 devices: a whole 2x2x4 slice. The times are simulated.
32 devices in a mesh: dp: 8 (over y, x, core), tensor: 4 (over z).
Axes of the slice: x: 2, y: 2, z: 4, core: 2. Of those that a mesh axis runs over, the one named last changes fastest.
Arguments:
- inputs: bfloat16 [32768, 768], P('dp'), may hold values from -6 to 6
- segments: int32 [64, 512], P('dp'), may hold values from 0 to 7, never falling along the last dimension, each value on 1 to 128 neighbouring positions
- w_query: bfloat16 [768, 768], P(None, 'tensor'), may hold values from -0.21875 to 0.21875
- w_key: bfloat16 [768, 768], P(None, 'tensor'), may hold values from -0.21875 to 0.21875
- w_value: bfloat16 [768, 768], P(None, 'tensor'), may hold values from -0.21875 to 0.21875
- b_query: bfloat16 [768], P('tensor'), may hold values from -3 to 3
- b_value: bfloat16 [768], P('tensor'), may hold values from -3 to 3
- w_output: bfloat16 [768, 768], P('tensor'), may hold values from -0.875 to 0.875
- b_output: bfloat16 [768], replicated, may hold values from -3 to 3
- gain_attn: bfloat16 [768], replicated, may hold values from 0.5 to 1.5
- shift_attn: bfloat16 [768], replicated, may hold values from -3 to 3
- w_hidden: bfloat16 [768, 3072], P(None, 'tensor'), may hold values from -0.21875 to 0.21875
- b_hidden: bfloat16 [3072], P('tensor'), may hold values from -3 to 3
- w_project: bfloat16 [3072, 768], P('tensor'), may hold values from -0.109375 to 0.109375
- b_project: bfloat16 [768], replicated, may hold values from -3 to 3
- gain_ffn: bfloat16 [768], replicated, may hold values from 0.5 to 1.5
- shift_ffn: bfloat16 [768], replicated, may hold values from -3 to 3
- cotangent: bfloat16 [32768, 768], P(('dp', 'tensor')), may hold values from -6 to 6
Outputs:
- output: bfloat16 [32768, 768], P(('dp', 'tensor'))
- grad_input: float32 [32768, 768], P(('dp', 'tensor'))
- grad_w_query: float32 [768, 768], P('dp', 'tensor')
- grad_w_key: float32 [768, 768], P('dp', 'tensor')
- grad_w_value: float32 [768, 768], P('dp', 'tensor')
- grad_w_output: float32 [768, 768], P('tensor', 'dp')
- grad_w_hidden: float32 [768, 3072], P('dp', 'tensor')
- grad_w_project: float32 [3072, 768], P('tensor', 'dp')
- grad_bias_qv: float32 [2, 12, 64], P(None, 'tensor', 'dp')
- grad_b_hidden: float32 [48, 64], P('tensor', 'dp')
- grad_vectors: float32 [6, 768], P(None, ('dp', 'tensor'))
Inputs may be any that keep to these rules, and one draw needn't show every extreme that they name: `segments`: within each row of 512 tokens segment numbers never fall; each text holds 1 to 128 tokens, and some text holds exactly 128.
All inputs are finite; a program needn't handle non-finite values.
Results may differ from a plain program's by a relative error of at most 0.014.
Values may be sent and summed in bfloat16 or wider, within the bound.
A program may use at most 192 MiB of HBM per device.

v0:
```python
import jax
import jax.numpy as jnp
from jax import lax
from jax.sharding import PartitionSpec as P

HD = 64
norm_epsilon = 1e-12
root_half = 0.7071067811865476


def norm_forward(values, norm_gain, norm_shift):
    average = jnp.mean(values, axis=-1, keepdims=True)
    centered = values - average
    variance = jnp.mean(centered * centered, axis=-1, keepdims=True)
    inverse = lax.rsqrt(variance + norm_epsilon)
    scaled = centered * inverse
    return (scaled * norm_gain + norm_shift, scaled, inverse)


def norm_backward(grad_out, scaled, inverse, norm_gain):
    weighted = grad_out * norm_gain
    mean_grad = jnp.mean(weighted, axis=-1, keepdims=True)
    mean_proj = jnp.mean(weighted * scaled, axis=-1, keepdims=True)
    return inverse * (weighted - mean_grad - scaled * mean_proj)


def gelu_exact(values):
    return 0.5 * values * (1.0 + lax.erf(values * root_half))


def cross_rows(left, right):
    return lax.dot_general(
        left, right, (((0,), (0,)), ((), ())), preferred_element_type=jnp.float32
    )


def times_transposed(left, right):
    return lax.dot_general(
        left, right, (((1,), (1,)), ((), ())), preferred_element_type=jnp.float32
    )


def masked_scores(queries, keys_in, segment_row):
    same_text = segment_row[:, None] == segment_row[None, :]
    scores = jnp.einsum("qhd,khd->hqk", queries, keys_in, preferred_element_type=jnp.float32)
    scores = scores * queries.shape[2] ** (-0.5)
    return jnp.where(same_text[None], scores, -1000000000.0)


def attend_forward(packed):
    queries, keys_in, values, segment_row = packed
    scores = masked_scores(queries, keys_in, segment_row)
    row_max = jnp.max(scores, axis=-1, keepdims=True)
    exponent = jnp.exp(scores - row_max)
    row_total = jnp.sum(exponent, axis=-1, keepdims=True)
    attn_probs = (exponent / row_total).astype(jnp.bfloat16)
    mixed_heads = jnp.einsum("hqk,khd->qhd", attn_probs, values, preferred_element_type=jnp.float32)
    return (mixed_heads.astype(jnp.bfloat16), row_max + jnp.log(row_total))


def attend_backward(packed):
    queries, keys_in, values, segment_row, logsum, grad_mixed = packed
    score_scale = queries.shape[2] ** (-0.5)
    scores = masked_scores(queries, keys_in, segment_row)
    attn_probs = jnp.exp(scores - logsum)
    grad_probs = jnp.einsum("qhd,khd->hqk", grad_mixed, values, preferred_element_type=jnp.float32)
    grad_values = jnp.einsum(
        "hqk,qhd->khd",
        attn_probs.astype(jnp.bfloat16),
        grad_mixed,
        preferred_element_type=jnp.float32,
    )
    inner_sum = jnp.sum(attn_probs * grad_probs, axis=-1, keepdims=True)
    grad_scores = (attn_probs * (grad_probs - inner_sum)).astype(jnp.bfloat16)
    grad_queries = (
        jnp.einsum("hqk,khd->qhd", grad_scores, keys_in, preferred_element_type=jnp.float32)
        * score_scale
    )
    grad_keys = (
        jnp.einsum("hqk,qhd->khd", grad_scores, queries, preferred_element_type=jnp.float32)
        * score_scale
    )
    return (
        grad_queries.astype(jnp.bfloat16),
        grad_keys.astype(jnp.bfloat16),
        grad_values.astype(jnp.bfloat16),
    )


def per_device(
    inputs,
    segments,
    w_query,
    w_key,
    w_value,
    b_query,
    b_value,
    w_output,
    b_output,
    gain_attn,
    shift_attn,
    w_hidden,
    b_hidden,
    w_project,
    b_project,
    gain_ffn,
    shift_ffn,
    cotangent,
):
    seq_len = segments.shape[1]
    share_tokens = cotangent.shape[0]
    share_rows = share_tokens // seq_len
    width = inputs.shape[1]
    groups, parts = (lax.axis_size("tensor"), lax.axis_size("dp"))
    place, part = (lax.axis_index("tensor"), lax.axis_index("dp"))
    everyone = ("tensor", "dp")
    low = jnp.bfloat16
    wide = jnp.float32

    def gathered(shard):
        rows = shard.shape[0] // parts
        piece = lax.dynamic_slice_in_dim(shard, part * rows, rows, 0)
        return lax.all_gather(piece, everyone, axis=0, tiled=True)

    def bias_of(shard):
        return lax.all_gather(shard, "tensor", axis=0, tiled=True).astype(wide)

    tokens = lax.dynamic_slice_in_dim(inputs, place * share_tokens, share_tokens, 0)
    rows_segments = lax.dynamic_slice_in_dim(segments, place * share_rows, share_rows, 0)
    split = w_query.shape[1]
    w_in = gathered(jnp.concatenate([w_query, w_key, w_value], axis=1))
    w_in = (
        w_in.reshape(groups, width, 3, split)
        .transpose(1, 2, 0, 3)
        .reshape(width, 3 * groups * split)
    )
    w_out = gathered(w_output)
    w_up = gathered(w_hidden).reshape(groups, width, -1).transpose(1, 0, 2).reshape(width, -1)
    w_down = gathered(w_project)
    small = bias_of(jnp.concatenate([b_query, b_value, b_hidden])).reshape(groups, -1)
    bias_query = small[:, :split].reshape(-1)
    bias_value = small[:, split : 2 * split].reshape(-1)
    bias_hidden = small[:, 2 * split :].reshape(-1)
    full = groups * split
    head_shape = (share_rows, seq_len, full // HD, HD)
    attn_gain = gain_attn.astype(wide)
    attn_shift = shift_attn.astype(wide)
    attn_bias = b_output.astype(wide)
    ffn_gain = gain_ffn.astype(wide)
    ffn_shift = shift_ffn.astype(wide)
    ffn_bias = b_project.astype(wide)
    grad_out = cotangent.astype(wide)
    projected = jnp.dot(tokens, w_in, preferred_element_type=wide)
    queries = (projected[:, :full] + bias_query).astype(low)
    keys_in = projected[:, full : 2 * full].astype(low)
    values = (projected[:, 2 * full :] + bias_value).astype(low)
    query_heads = queries.reshape(head_shape)
    key_heads = keys_in.reshape(head_shape)
    value_heads = values.reshape(head_shape)
    mixed_heads, logsum = lax.map(
        attend_forward, (query_heads, key_heads, value_heads, rows_segments)
    )
    mixed = mixed_heads.reshape(share_tokens, full)
    hidden = tokens.astype(wide) + (jnp.dot(mixed, w_out, preferred_element_type=wide) + attn_bias)
    normed, scaled, inverse = norm_forward(hidden, attn_gain, attn_shift)
    normed_low = normed.astype(low)
    hidden_pre = jnp.dot(normed_low, w_up, preferred_element_type=wide) + bias_hidden
    active, gelu_pull = jax.vjp(gelu_exact, hidden_pre)
    active_low = active.astype(low)
    block_sum = normed + (jnp.dot(active_low, w_down, preferred_element_type=wide) + ffn_bias)
    output, scaled_out, inverse_out = norm_forward(block_sum, ffn_gain, ffn_shift)
    grad_sum = norm_backward(grad_out, scaled_out, inverse_out, ffn_gain)
    grad_ffn_gain = jnp.sum(grad_out * scaled_out, axis=0)
    grad_ffn_shift = jnp.sum(grad_out, axis=0)
    grad_sum_low = grad_sum.astype(low)
    grad_ffn_bias = jnp.sum(grad_sum_low.astype(wide), axis=0)
    grad_active = times_transposed(grad_sum_low, w_down)
    grad_w_down = cross_rows(grad_sum_low, active_low)
    grad_hidden_pre = gelu_pull(grad_active)[0].astype(low)
    grad_b_hidden = jnp.sum(grad_hidden_pre.astype(wide), axis=0)
    grad_w_up = cross_rows(normed_low, grad_hidden_pre)
    grad_normed = grad_sum + times_transposed(grad_hidden_pre, w_up)
    grad_hidden = norm_backward(grad_normed, scaled, inverse, attn_gain)
    grad_hidden_low = grad_hidden.astype(low)
    grad_attn_gain = jnp.sum(grad_normed * scaled, axis=0)
    grad_attn_shift = jnp.sum(grad_normed, axis=0)
    grad_attn_bias = jnp.sum(grad_hidden_low.astype(wide), axis=0)
    grad_w_out = cross_rows(grad_hidden_low, mixed)
    grad_mixed = times_transposed(grad_hidden_low, w_out).astype(low).reshape(head_shape)
    grad_q, grad_k, grad_v = lax.map(
        attend_backward, (query_heads, key_heads, value_heads, rows_segments, logsum, grad_mixed)
    )
    grad_q = grad_q.reshape(share_tokens, full)
    grad_k = grad_k.reshape(share_tokens, full)
    grad_v = grad_v.reshape(share_tokens, full)
    grad_projected = jnp.concatenate([grad_q, grad_k, grad_v], axis=1)
    grad_w_in = cross_rows(tokens, grad_projected)
    grad_b_query = jnp.sum(grad_q.astype(wide), axis=0)
    grad_b_value = jnp.sum(grad_v.astype(wide), axis=0)
    grad_input = grad_hidden + times_transposed(grad_projected, w_in)

    def scattered(grad):
        rows = grad.shape[0]
        grad = grad.reshape(rows, groups, -1).transpose(1, 0, 2).reshape(groups * rows, -1)
        return lax.psum_scatter(grad, everyone, scatter_dimension=0, tiled=True)

    sum_down = scattered(grad_w_down).T
    sum_up = scattered(grad_w_up)
    sum_out = scattered(grad_w_out).T
    sum_in = scattered(
        grad_w_in.reshape(width, 3, groups, split).transpose(0, 2, 1, 3).reshape(width, -1)
    )
    vectors = jnp.concatenate(
        [
            jnp.stack([grad_b_query, grad_b_value]).reshape(2 * groups, split),
            grad_b_hidden.reshape(-1, split),
            jnp.stack(
                [
                    grad_attn_gain,
                    grad_attn_shift,
                    grad_attn_bias,
                    grad_ffn_gain,
                    grad_ffn_shift,
                    grad_ffn_bias,
                ]
            ).reshape(-1, split),
        ],
        axis=0,
    )
    vectors = lax.psum(vectors, ("dp", "tensor"))
    bias_qv = vectors[: 2 * groups].reshape(2, groups, split // HD, HD)
    rest = vectors[2 * groups :]
    hid = bias_hidden.shape[0] // split
    bias_h = rest[:hid].reshape(groups, -1, HD)
    vec = rest[hid:].reshape(6, -1)
    piece = HD // parts
    bias_qv = lax.dynamic_slice_in_dim(bias_qv, place, 1, 1)[:, 0]
    bias_qv = lax.dynamic_slice_in_dim(bias_qv, part * piece, piece, 2)
    bias_h = lax.dynamic_slice_in_dim(bias_h, place, 1, 0)[0]
    bias_h = lax.dynamic_slice_in_dim(bias_h, part * piece, piece, 1)
    piece = width // (parts * groups)
    vec = lax.dynamic_slice_in_dim(vec, (part * groups + place) * piece, piece, 1)
    return (
        output.astype(low),
        grad_input,
        sum_in[:, :split],
        sum_in[:, split : 2 * split],
        sum_in[:, 2 * split :],
        sum_out,
        sum_up,
        sum_down,
        bias_qv,
        bias_h,
        vec,
    )


def solution(mesh):
    in_specs = (
        P("dp", None),
        P("dp", None),
        P(None, "tensor"),
        P(None, "tensor"),
        P(None, "tensor"),
        P("tensor"),
        P("tensor"),
        P("tensor", None),
        P(),
        P(),
        P(),
        P(None, "tensor"),
        P("tensor"),
        P("tensor", None),
        P(),
        P(),
        P(),
        P(("dp", "tensor"), None),
    )
    out_specs = (
        P(("dp", "tensor"), None),
        P(("dp", "tensor"), None),
        P("dp", "tensor"),
        P("dp", "tensor"),
        P("dp", "tensor"),
        P("tensor", "dp"),
        P("dp", "tensor"),
        P("tensor", "dp"),
        P(None, "tensor", "dp"),
        P("tensor", "dp"),
        P(None, ("dp", "tensor")),
    )
    return jax.shard_map(
        per_device, mesh=mesh, in_specs=in_specs, out_specs=out_specs, check_vma=False
    )
```

profile of v0, /device:TPU:0, one launch (start us, length us, event | category | flops | bytes accessed | tf_op | source)
XLA Modules:
  0.0 852.2 jit_solution(8184249609554273054)
XLA Ops:
  18.6 14.9 %all-gather = bf16[4,1,1152]{2,1,0:T(2,128)(2,1)S(1)} all-gather(bf16[1,1,1152]{2,1,0:T(2,128)(2,1)S(1)} %reshape.275), channel_id=1, replica_groups=mesh['dp'=8,'tensor'=4] {'tensor'}, dimensions={0}, use_global_device_ids=true | all-gather | bytes 11520 | tf_op jit(solution)/shard_map/all_gather | solution.py:126
  45.4 31.5 %all-gather.6.cloned.1.call-done = bf16[3072,576]{1,0:T(8,128)(2,1)} async-done(((bf16[96,576]{1,0:T(8,128)(2,1)}), bf16[3072,576]{1,0:T(8,128)(2,1)}) %all-gather.6.cloned.1.call-update) | async-done | bytes 3538960 | tf_op jit(solution)/shard_map/all_gather | solution.py:123
  76.9 6.0 copy.132
  82.9 7.7 reshape.246
  93.2 3.9 fusion.82
  109.1 3.9 reshape.252
  118.4 3.9 reshape.250
  126.5 23.2 %while.26 = (s32[]{:T(128)}, bf16[2,512,12,64]{1,3,2,0:T(8,128)(2,1)}, f32[2,12,512,1]{2,1,3,0:T(8,128)S(1)}, bf16[2,512,12,64]{1,3,2,0:T(8,128)(2,1)}, s32[2,51...) while((s32[]{:T(128)}, ...), condition=%wide.region_3.4_spmd, body=%wide.region_0.3_spmd.sunk | while | flops 843704320 | bytes 42172516 | solution.py:160
  126.9 3.2 fusion.124
  132.7 5.5 fusion.126
  138.4 3.2 fusion.124
  144.2 5.5 fusion.126
  154.3 3.9 fusion.80
  160.3 38.9 %all-gather.10.cloned.1.call-done = bf16[3072,768]{1,0:T(8,128)(2,1)} async-done(((bf16[96,768]{1,0:T(8,128)(2,1)}), bf16[3072,768]{1,0:T(8,128)(2,1)}) %all-gather.10.cloned.1.call-update) | async-done | bytes 4718608 | tf_op jit(solution)/shard_map/all_gather | solution.py:123
  199.2 6.8 copy.141
  206.0 13.7 %multiply_convert_fusion.3 = (bf16[1024,3072]{1,0:T(8,128)(2,1)}, f32[1024,3072]{1,0:T(8,128)}) fusion(f32[3072]{0:T(1024)S(1)} %copy-done.34, bf16[768,3072]{0,1:T(8,128)(2,1)} %bitcast.212, f32[1024,768]{0,1:T(8,128)} %copy-done.9, f32[768]{0:T(1024)S(1)} %copy-done.37, f32[768]{0:T(1024)S(1)} %copy-done.26, f32[1024]{0:T(1024)S(1)} %add_rsqrt_fusion.1, ...), kind=kOutput, calls=%fused_computation.66 | convolution fusion | flops 4854644736 | bytes 26765312 | tf_op jit(solution)/shard_map/dot_general | solution.py:167
  219.7 44.8 %all-gather.12.cloned.1.call-done = bf16[3072,768]{1,0:T(8,128)(2,1)} async-done(((bf16[96,768]{1,0:T(8,128)(2,1)}), bf16[3072,768]{1,0:T(8,128)(2,1)}) %all-gather.12.cloned.1.call-update) | async-done | bytes 4718608 | tf_op jit(solution)/shard_map/all_gather | solution.py:123
  264.5 9.4 %fusion.81 = (f32[1024]{0:T(1024)S(1)}, f32[1024,768]{0,1:T(8,128)S(1)}) fusion(f32[768]{0:T(1024)S(1)} %copy-done.39, bf16[1024,3072]{1,0:T(8,128)(2,1)} %get-tuple-element.280, bf16[3072,768]{1,0:T(8,128)(2,1)} %all-gather.12.cloned.1.call-done, f32[768]{0:T(1024)S(1)} %copy-done.37, f32[768]{0:T(1024)S(1)} %copy-done.26, f32[1024]{0:T(1024)S(1)} %add_rsqrt_fusion.1, ...), kind=kOutput, calls=%fused_computation.141 | convolution fusion | flops 4837342208 | bytes 17323008 | tf_op jit(solution)/shard_map/dot_general | solution.py:170
  277.3 3.3 convert_reduce_fusion.2
  280.6 15.2 %convert_reduce_fusion = (f32[3072]{0:T(1024)}, bf16[1024,3072]{1,0:T(8,128)(2,1)}) fusion(bf16[1024,768]{0,1:T(8,128)(2,1)S(1)} %get-tuple-element.263, bf16[3072,768]{1,0:T(8,128)(2,1)S(1)} %copy-done.45, f32[1024,3072]{1,0:T(8,128)} %get-tuple-element.281, f32[3072]{0:T(1024)S(1)} %copy-done.34), kind=kOutput, calls=%fused_computation.64 | convolution fusion | flops 4882166784 | bytes 25190400 | tf_op jit(solution)/shard_map/dot_general | solution.py:38
  295.9 11.2 %multiply_reduce_fusion.1 = (f32[768]{0:T(1024)}, f32[1024]{0:T(1024)S(1)}, f32[1024]{0:T(1024)S(1)}, f32[768]{0:T(1024)}, f32[1024,768]{0,1:T(8,128)}) fusion(f32[1024,768]{0,1:T(8,128)S(1)} %copy-done.10, f32[1024]{0:T(1024)S(1)} %add_rsqrt_fusion.1, f32[1024]{0:T(1024)S(1)} %broadcast_multiply_fusion.5, f32[768]{0:T(1024)S(1)} %copy-done.26, ...), kind=kOutput, calls=%fused_computation.85 | convolution fusion | flops 4845989888 | bytes 22065152 | tf_op jit(solution)/shard_map/dot_general | solution.py:38
  307.1 3.7 convert_reduce_fusion.3
  317.8 3.8 reshape.256
  324.7 4.3 convolution_bitcast_fusion
  329.0 3.4 copy.183
  336.5 52.0 %while.27 = (s32[]{:T(128)}, bf16[2,512,12,64]{1,3,2,0:T(8,128)(2,1)}, bf16[2,512,12,64]{1,3,2,0:T(8,128)(2,1)}, bf16[2,512,12,64]{1,3,2,0:T(8,128)(2,1)}, bf16[...) while((s32[]{:T(128)}, ...), condition=%wide.region_14.15_spmd, body=%wide.region_12.14_spmd.sunk | while | flops 2062673920 | bytes 147524944 | solution.py:190
  340.0 3.9 fusion.138
  344.0 6.8 multiply_reduce_fusion.7
  350.8 7.3 multiply_convert_fusion.5
  365.8 4.0 fusion.138
  369.8 6.9 multiply_reduce_fusion.7
  376.7 7.2 multiply_convert_fusion.5
  391.9 3.2 copy.152
  399.1 3.9 fusion.84
  403.0 3.3 copy.155
  406.4 8.4 copy.182
  415.5 10.8 %fusion.73 = f32[768,3072]{1,0:T(8,128)} fusion(bf16[1024,3072]{1,0:T(8,128)(2,1)} %get-tuple-element.286, f32[1024,768]{0,1:T(8,128)} %copy-done.9, f32[768]{0:T(1024)S(1)} %copy-done.38, f32[768]{0:T(1024)S(1)} %copy-done.27, f32[1024]{0:T(1024)S(1)} %copy-done.29, f32[1024]{0:T(1024)S(1)} %copy-done.22), kind=kOutput, calls=%fused_computation.136 | convolution fusion | flops 4835770368 | bytes 18888704 | tf_op jit(solution)/shard_map/dot_general | solution.py:32
  426.3 12.5 %reshape.263 = f32[768,4,768]{2,1,0:T(4,128)} reshape(f32[768,3072]{1,0:T(8,128)} %fusion.73) | data formatting | bytes 18874368 | tf_op jit(solution)/shard_map/reshape | solution.py:204
  438.8 9.2 %copy.159 = f32[4,768,768]{2,1,0:T(8,128)} copy(f32[4,768,768]{2,0,1:T(4,128)} %bitcast.197) | data formatting | bytes 18874368 | tf_op jit(solution)/shard_map/transpose | solution.py:204
  448.0 10.0 %fusion.83 = f32[768,3072]{1,0:T(8,128)} fusion(bf16[1024,768]{0,1:T(8,128)(2,1)} %copy-done.19, bf16[1024,3072]{1,0:T(8,128)(2,1)} %get-tuple-element.280), kind=kOutput, calls=%fused_computation.143 | convolution fusion | flops 4831838208 | bytes 17301504 | tf_op jit(solution)/shard_map/dot_general | solution.py:32
  458.0 12.7 %reshape.265 = f32[768,4,768]{2,1,0:T(4,128)} reshape(f32[768,3072]{1,0:T(8,128)} %fusion.83) | data formatting | bytes 18874368 | tf_op jit(solution)/shard_map/reshape | solution.py:204
  470.8 9.5 %copy.160 = f32[4,768,768]{2,1,0:T(8,128)} copy(f32[4,768,768]{2,0,1:T(4,128)} %bitcast.198) | data formatting | bytes 18874368 | tf_op jit(solution)/shard_map/transpose | solution.py:204
  483.5 41.2 %psum.7 = f32[48,192]{1,0:T(8,128)S(1)} all-reduce(f32[48,192]{1,0:T(8,128)S(1)} %pad_maximum_fusion), channel_id=1, replica_groups=mesh['dp'=8,'tensor'=4] {'dp','tensor'}, use_global_device_ids=true, to_apply=%region_28.29 | all-reduce | flops 9216 | bytes 73728 | tf_op jit(solution)/shard_map/psum | solution.py:230
  528.9 10.0 %convolution_add_fusion.1 = f32[1024,768]{0,1:T(8,128)} fusion(f32[1024,768]{0,1:T(8,128)} %copy-done.16, bf16[1024,2304]{0,1:T(8,128)(2,1)} %copy-done.20, bf16[768,2304]{0,1:T(8,128)(2,1)} %bitcast.217), kind=kOutput, calls=%fused_computation.101 | convolution fusion | flops 3624665088 | bytes 14548992 | tf_op jit(solution)/shard_map/dot_general | solution.py:38
  538.9 3.5 copy.164
  544.8 16.7 %reduce-scatter.13.cloned.1.call-done = f32[96,576]{1,0:T(8,128)} async-done(((f32[3072,576]{1,0:T(8,128)}), f32[96,576]{1,0:T(8,128)}) %reduce-scatter.13.cloned.1.call-update) | async-done | bytes 221200
  563.2 139.7 %reduce-scatter.9.cloned.1.call-done = f32[96,768]{1,0:T(8,128)} async-done(((f32[3072,768]{1,0:T(8,128)}), f32[96,768]{1,0:T(8,128)}) %reduce-scatter.9.cloned.1.call-update) | async-done | bytes 294928 | tf_op jit(solution)/shard_map/reduce_scatter | solution.py:205
  703.0 141.8 %reduce-scatter.11.cloned.1.call-done = f32[96,768]{1,0:T(8,128)} async-done(((f32[3072,768]{1,0:T(8,128)}), f32[96,768]{1,0:T(8,128)}) %reduce-scatter.11.cloned.1.call-update) | async-done | bytes 294928 | tf_op jit(solution)/shard_map/reduce_scatter | solution.py:205
  (244 shorter events, 111.9 us)
Async XLA Ops:
  7.2 7.5 copy-start
  7.2 9.9 %copy-start.41 = (bf16[768]{0:T(1024)(128)(2,1)S(1)}, bf16[768]{0:T(1024)(128)(2,1)}, u32[]{:S(2)}) copy-start(bf16[768]{0:T(1024)(128)(2,1)} %param.34) | copy-start | bytes 4612
  7.2 26.3 %copy-start.42 = (bf16[768]{0:T(1024)(128)(2,1)S(1)}, bf16[768]{0:T(1024)(128)(2,1)}, u32[]{:S(2)}) copy-start(bf16[768]{0:T(1024)(128)(2,1)} %param.31) | copy-start | bytes 4612
  7.2 26.9 %copy-start.43 = (bf16[768]{0:T(1024)(128)(2,1)S(1)}, bf16[768]{0:T(1024)(128)(2,1)}, u32[]{:S(2)}) copy-start(bf16[768]{0:T(1024)(128)(2,1)} %param.32) | copy-start | bytes 4612
  7.2 27.5 %copy-start.44 = (bf16[768]{0:T(1024)(128)(2,1)S(1)}, bf16[768]{0:T(1024)(128)(2,1)}, u32[]{:S(2)}) copy-start(bf16[768]{0:T(1024)(128)(2,1)} %param.37) | copy-start | bytes 4612
  7.2 32.7 %copy-start.18 = (bf16[1024,768]{1,0:T(8,128)(2,1)S(1)}, bf16[1024,768]{1,0:T(8,128)(2,1)}, u32[]{:S(2)}) copy-start(bf16[1024,768]{1,0:T(8,128)(2,1)} %param.39) | copy-start | bytes 4718596
  7.2 69.7 %all-gather.6.cloned.1.call-start = ((), (), s32[]{:S(2)}) async-start(), calls=%async_computation.4 | async-start | bytes 4055040 | tf_op jit(solution)/shard_map/all_gather | solution.py:123
  13.2 141.2 %all-gather.8.cloned.1.call-start = ((), (), s32[]{:S(2)}) async-start(), calls=%async_computation.5 | async-start | bytes 1216512 | tf_op jit(solution)/shard_map/all_gather | solution.py:123
  14.6 184.6 %all-gather.10.cloned.1.call-start = ((), (), s32[]{:S(2)}) async-start(), calls=%async_computation.6 | async-start | bytes 4866048 | tf_op jit(solution)/shard_map/all_gather | solution.py:123
  15.4 249.1 %all-gather.12.cloned.1.call-start = ((), (), s32[]{:S(2)}) async-start(), calls=%async_computation.7 | async-start | bytes 4866048 | tf_op jit(solution)/shard_map/all_gather | solution.py:123
  17.1 526.1 %reduce-scatter.15.cloned.1.call-start = ((), (), s32[]{:S(2)}) async-start(), calls=%async_computation.11 | async-start | bytes 3244032
  43.1 50.1 %copy-start.13 = (bf16[1024,768]{1,0:T(8,128)(2,1)}, bf16[1024,768]{1,0:T(8,128)(2,1)S(1)}, u32[]{:S(2)}) copy-start(bf16[1024,768]{1,0:T(8,128)(2,1)S(1)} %constant_dynamic-slice_fusion.9) | copy-start | bytes 4718596
  93.2 3.9 copy-start.15
  149.7 4.6 copy-start.40
  158.2 1.7 copy-start.9
  158.3 148.9 %copy-start.21 = (f32[1024]{0:T(1024)}, f32[1024]{0:T(1024)S(1)}, u32[]{:S(2)}) copy-start(f32[1024]{0:T(1024)S(1)} %broadcast_multiply_fusion.5) | copy-start | bytes 12292
  160.3 146.8 %copy-start.28 = (f32[1024]{0:T(1024)}, f32[1024]{0:T(1024)S(1)}, u32[]{:S(2)}) copy-start(f32[1024]{0:T(1024)S(1)} %add_rsqrt_fusion.1) | copy-start | bytes 12292
  199.2 6.8 copy-start.26
  199.2 6.8 copy-start.34
  199.2 6.8 copy-start.37
  206.0 58.5 %copy-start.39 = (f32[768]{0:T(1024)S(1)}, f32[768]{0:T(1024)}, u32[]{:S(2)}) copy-start(f32[768]{0:T(1024)} %convert_element_type.111) | copy-start | bytes 9220
  273.9 1.4 copy-start.8
  274.4 3.0 copy-start.30
  275.4 5.2 copy-start.45
  277.3 18.5 %slice-start = ((s8[4718592]{0:T(1024)(128)(4,1)}), s8[4194304]{0:T(1024)(128)(4,1)S(1)}, s32[]{:S(2)}) async-start(s8[4718592]{0:T(1024)(128)(4,1)} %bitcast.213), calls=%async_computation.12 | async-start | bytes 8388608
  280.6 15.3 %copy-start.19 = (bf16[1024,768]{0,1:T(8,128)(2,1)}, bf16[1024,768]{0,1:T(8,128)(2,1)S(1)}, u32[]{:S(2)}) copy-start(bf16[1024,768]{0,1:T(8,128)(2,1)S(1)} %get-tuple-element.263) | copy-start | bytes 4718596
  280.6 15.3 %copy-start.10 = (f32[1024,768]{0,1:T(8,128)S(1)}, f32[1024,768]{0,1:T(8,128)}, u32[]{:S(2)}) copy-start(f32[1024,768]{0,1:T(8,128)} %copy-done.9) | copy-start | bytes 9437188
  280.6 15.3 %slice-start.1 = ((s8[4718592]{0:T(1024)(128)(4,1)}), s8[524288]{0:T(1024)(128)(4,1)S(1)}, s32[]{:S(2)}) async-start(s8[4718592]{0:T(1024)(128)(4,1)} %bitcast.213), calls=%async_computation.13 | async-start | bytes 1048576
  307.1 5.5 copy-start.46
  310.9 1.7 copy-start.16
  321.6 3.1 copy-start.17
  332.5 229.0 %reduce-scatter.13.cloned.1.call-start = ((), (), s32[]{:S(2)}) async-start(), calls=%async_computation.10 | async-start | bytes 8110080
  336.9 3.1 copy-start.4
  340.0 4.0 copy-start.3
  350.8 7.3 copy-start.11
  358.1 2.0 copy-start.2
  358.1 2.0 copy-start.5
  362.7 3.1 copy-start.4
  365.8 4.0 copy-start.3
  376.7 7.2 copy-start.11
  383.9 2.0 copy-start.2
  383.9 2.0 copy-start.5
  391.9 3.6 copy-start.7
  397.7 1.4 copy-start.14
  399.1 3.9 copy-start.20
  414.8 288.2 %reduce-scatter.9.cloned.1.call-start = ((), (), s32[]{:S(2)}) async-start(), calls=%async_computation.8 | async-start | bytes 9732096 | tf_op jit(solution)/shard_map/reduce_scatter | solution.py:205
  448.0 396.8 %reduce-scatter.11.cloned.1.call-start = ((), (), s32[]{:S(2)}) async-start(), calls=%async_computation.9 | async-start | bytes 9732096 | tf_op jit(solution)/shard_map/reduce_scatter | solution.py:205
  528.9 315.9 %copy-start.1 = (bf16[768,768]{1,0:T(8,128)(2,1)S(1)}, bf16[768,768]{1,0:T(8,128)(2,1)}, u32[]{:S(2)}) copy-start(bf16[768,768]{1,0:T(8,128)(2,1)} %param.33) | copy-start | bytes 3538948
  (16 other events, 13.8 us)
Sparse Core Ops, SparseCore 0:
  13.3 63.5 all-gather.5
  80.4 52.7 all-gather.7
  136.7 62.4 all-gather.9
  202.5 61.9 all-gather.11
  332.6 100.4 reduce-scatter.14
  438.6 122.7 reduce-scatter.12
  567.9 135.0 reduce-scatter.8
  709.5 135.3 reduce-scatter.10
where the time goes:
time: 862 us; the launch traced here: 852 us
  waiting for transfers between devices  414 us (48%)
  local copies, waits for them, and re-layouts  174 us (20%)
  matrix products  150 us (17%)
  blocking collectives  56.1 us (7%)
  other arithmetic  41.7 us (5%)
  between operations  15.3 us (2%)
    reduce_scatter x2, waiting for transfers between devices, scattered(): return lax.psum_scatter(grad, everyone, scatter_dimension=0, tiled=True)  282 us
    all_gather x4, waiting for transfers between devices, gathered(): return lax.all_gather(piece, everyone, axis=0, tiled=True)  115 us
    psum x1, blocking collectives, per_device(): vectors = lax.psum(vectors, ('dp', 'tensor'))  41.2 us
    dot_general x4, matrix products, times_transposed(): lax.dot_general(left, right, (((1,), (1,)), ((), ())), preferred_element_...  39.1 us
    unnamed x103, local copies, waits for them, and re-layouts  38.6 us
    dot_general x4, matrix products, cross_rows(): lax.dot_general(left, right, (((0,), (0,)), ((), ())), preferred_element_...  29 us
    reshape x2, local copies, waits for them, and re-layouts, scattered(): grad.reshape(rows, groups, -1).transpose(1, 0, 2).reshape(groups * rows, -1)  25.2 us
    transpose x2, local copies, waits for them, and re-layouts, scattered(): grad.reshape(rows, groups, -1).transpose(1, 0, 2).reshape(groups * rows, -1)  18.7 us
  transfers between devices with their start and end apart: 8, of which 6 were waited for; matrix products, arithmetic and copies ran while one was open for 34% of the time, Pallas kernels for 0%

commit v1 on v0

--- a/solution.py
+++ b/solution.py
@@ -227,7 +227,7 @@
         ],
         axis=0,
     )
-    vectors = lax.psum(vectors, ("dp", "tensor"))
+    vectors = lax.all_gather(vectors, ("dp", "tensor")).sum(axis=0)
     bias_qv = vectors[: 2 * groups].reshape(2, groups, split // HD, HD)
     rest = vectors[2 * groups :]
     hid = bias_hidden.shape[0] // split

time: 862 us -> 973 us (1.13)
  waiting for transfers between devices: 414 us -> 565 us
  blocking collectives: 56.1 us -> 14.9 us
    unnamed x10 -> x11, waiting for transfers between devices: 16.8 us -> 168 us
    psum x1 -> x0, blocking collectives: 41.2 us -> none  [per_device(): vectors = lax.psum(vectors, ('dp', 'tensor'))]
    unnamed x103 -> x93, local copies, waits for them, and re-layouts: 38.6 us -> 36.6 us
  transfers between devices with their start and end apart: 8 -> 9, of which waited for: 6 -> 7; matrix products, arithmetic and copies ran while one was open for 34% -> 24% of each run, Pallas kernels for 0% -> 0%
where the time goes in v1:
time: 973 us; the launch traced here: 963 us
  waiting for transfers between devices  565 us (58%)
  local copies, waits for them, and re-layouts  171 us (18%)
  matrix products  151 us (16%)
  other arithmetic  44.7 us (5%)
  blocking collectives  14.9 us (2%)
  between operations  14.6 us (2%)
    reduce_scatter x2, waiting for transfers between devices, scattered(): return lax.psum_scatter(grad, everyone, scatter_dimension=0, tiled=True)  281 us
    unnamed x11, waiting for transfers between devices  168 us
    all_gather x4, waiting for transfers between devices, gathered(): return lax.all_gather(piece, everyone, axis=0, tiled=True)  115 us
    dot_general x4, matrix products, times_transposed(): lax.dot_general(left, right, (((1,), (1,)), ((), ())), preferred_element_...  40.2 us
    unnamed x93, local copies, waits for them, and re-layouts  36.6 us
    dot_general x4, matrix products, cross_rows(): lax.dot_general(left, right, (((0,), (0,)), ((), ())), preferred_element_...  28.4 us
    reshape x2, local copies, waits for them, and re-layouts, scattered(): grad.reshape(rows, groups, -1).transpose(1, 0, 2).reshape(groups * rows, -1)  25 us
  transfers between devices with their start and end apart: 9, of which 7 were waited for; matrix products, arithmetic and copies ran while one was open for 24% of the time, Pallas kernels for 0%

profile of v1, /device:TPU:0, one launch (start us, length us, event | category | flops | bytes accessed | tf_op | source)
XLA Modules:
  0.0 962.9 jit_solution(15766987510544026565)
XLA Ops:
  18.6 14.9 %all-gather.1 = bf16[4,1,1152]{2,1,0:T(2,128)(2,1)S(1)} all-gather(bf16[1,1,1152]{2,1,0:T(2,128)(2,1)S(1)} %reshape.276), channel_id=1, replica_groups=mesh['dp'=8,'tensor'=4] {'tensor'}, dimensions={0}, use_global_device_ids=true | all-gather | bytes 11520 | tf_op jit(solution)/shard_map/all_gather | solution.py:126
  45.4 31.5 %all-gather.8.cloned.1.call-done = bf16[3072,576]{1,0:T(8,128)(2,1)} async-done(((bf16[96,576]{1,0:T(8,128)(2,1)}), bf16[3072,576]{1,0:T(8,128)(2,1)}) %all-gather.8.cloned.1.call-update) | async-done | bytes 3538960 | tf_op jit(solution)/shard_map/all_gather | solution.py:123
  76.9 6.0 copy.176
  82.9 7.7 reshape.246
  93.1 3.9 fusion.82
  109.0 3.9 reshape.252
  118.4 3.9 reshape.250
  126.5 23.2 %while.26 = (s32[]{:T(128)}, bf16[2,512,12,64]{1,3,2,0:T(8,128)(2,1)}, f32[2,12,512,1]{2,1,3,0:T(8,128)S(1)}, bf16[2,512,12,64]{1,3,2,0:T(8,128)(2,1)}, s32[2,51...) while((s32[]{:T(128)}, ...), condition=%wide.region_3.4_spmd, body=%wide.region_0.3_spmd.sunk | while | flops 843704320 | bytes 42172516 | solution.py:160
  126.9 3.2 fusion.124
  132.7 5.5 fusion.126
  138.4 3.2 fusion.124
  144.2 5.5 fusion.126
  154.4 3.9 fusion.80
  160.3 38.9 %all-gather.12.cloned.1.call-done = bf16[3072,768]{1,0:T(8,128)(2,1)} async-done(((bf16[96,768]{1,0:T(8,128)(2,1)}), bf16[3072,768]{1,0:T(8,128)(2,1)}) %all-gather.12.cloned.1.call-update) | async-done | bytes 4718608 | tf_op jit(solution)/shard_map/all_gather | solution.py:123
  199.2 6.7 copy.185
  205.9 13.7 %multiply_convert_fusion.3 = (bf16[1024,3072]{1,0:T(8,128)(2,1)}, f32[1024,3072]{1,0:T(8,128)}) fusion(f32[3072]{0:T(1024)S(1)} %copy-done.32, bf16[768,3072]{0,1:T(8,128)(2,1)} %bitcast.213, f32[1024,768]{0,1:T(8,128)} %copy-done.9, f32[768]{0:T(1024)S(1)} %copy-done.33, f32[768]{0:T(1024)S(1)} %copy-done.27, f32[1024]{0:T(1024)S(1)} %add_rsqrt_fusion.1, ...), kind=kOutput, calls=%fused_computation.66 | convolution fusion | flops 4854644736 | bytes 26765312 | tf_op jit(solution)/shard_map/dot_general | solution.py:167
  219.6 44.8 %all-gather.14.cloned.1.call-done = bf16[3072,768]{1,0:T(8,128)(2,1)} async-done(((bf16[96,768]{1,0:T(8,128)(2,1)}), bf16[3072,768]{1,0:T(8,128)(2,1)}) %all-gather.14.cloned.1.call-update) | async-done | bytes 4718608 | tf_op jit(solution)/shard_map/all_gather | solution.py:123
  264.5 9.4 fusion.81
  279.4 14.7 %convert_reduce_fusion = (f32[3072]{0:T(1024)S(1)}, bf16[1024,3072]{1,0:T(8,128)(2,1)}) fusion(bf16[1024,768]{0,1:T(8,128)(2,1)S(1)} %get-tuple-element.291, bf16[3072,768]{1,0:T(8,128)(2,1)S(1)} %copy-done.41, f32[1024,3072]{1,0:T(8,128)} %get-tuple-element.309, f32[3072]{0:T(1024)S(1)} %copy-done.32), kind=kOutput, calls=%fused_computation.64 | convolution fusion | flops 4882166784 | bytes 25190400 | tf_op jit(solution)/shard_map/dot_general | solution.py:38
  294.1 10.6 %multiply_reduce_fusion.1 = (f32[768]{0:T(1024)S(1)}, f32[1024]{0:T(1024)S(1)}, f32[1024]{0:T(1024)S(1)}, f32[768]{0:T(1024)S(1)}, f32[1024,768]{0,1:T(8,128)}) fusion(f32[1024,768]{0,1:T(8,128)S(1)} %copy-done.10, f32[1024]{0:T(1024)S(1)} %add_rsqrt_fusion.1, f32[1024]{0:T(1024)S(1)} %broadcast_multiply_fusion.5, f32[768]{0:T(1024)S(1)} %copy-done.27, ...), kind=kOutput, calls=%fused_computation.85 | convolution fusion | flops 4845989888 | bytes 22065152 | tf_op jit(solution)/shard_map/dot_general | solution.py:38
  304.8 4.7 convert_reduce_fusion.3
  310.9 4.9 convolution_convert_fusion
  318.4 3.9 reshape.256
  329.2 51.7 %while.27 = (s32[]{:T(128)}, bf16[2,512,12,64]{1,3,2,0:T(8,128)(2,1)}, bf16[2,512,12,64]{1,3,2,0:T(8,128)(2,1)}, bf16[2,512,12,64]{1,3,2,0:T(8,128)(2,1)}, bf16[...) while((s32[]{:T(128)}, ...), condition=%wide.region_14.15_spmd, body=%wide.region_12.14_spmd.sunk | while | flops 2062673920 | bytes 147524944 | solution.py:190
  329.7 3.1 fusion.135
  332.8 4.0 fusion.138
  336.8 6.9 multiply_reduce_fusion.7
  343.6 7.1 multiply_convert_fusion.5
  358.5 4.0 fusion.138
  362.5 6.9 multiply_reduce_fusion.7
  369.4 7.1 multiply_convert_fusion.5
  385.3 3.8 convolution_bitcast_fusion
  391.9 3.2 copy.196
  401.1 3.9 fusion.84
  405.0 3.4 copy.199
  408.4 8.3 copy.226
  417.4 10.5 %fusion.73 = f32[768,3072]{1,0:T(8,128)} fusion(bf16[1024,3072]{1,0:T(8,128)(2,1)} %get-tuple-element.314, f32[1024,768]{0,1:T(8,128)} %copy-done.9, f32[768]{0:T(1024)S(1)} %copy-done.34, f32[768]{0:T(1024)S(1)} %copy-done.28, f32[1024]{0:T(1024)S(1)} %copy-done.30, f32[1024]{0:T(1024)S(1)} %copy-done.25), kind=kOutput, calls=%fused_computation.136 | convolution fusion | flops 4835770368 | bytes 18888704 | tf_op jit(solution)/shard_map/dot_general | solution.py:32
  427.9 12.4 %reshape.263 = f32[768,4,768]{2,1,0:T(4,128)} reshape(f32[768,3072]{1,0:T(8,128)} %fusion.73) | data formatting | bytes 18874368 | tf_op jit(solution)/shard_map/reshape | solution.py:204
  440.3 9.2 copy.203
  450.9 10.2 %fusion.83 = f32[768,3072]{1,0:T(8,128)} fusion(bf16[1024,768]{0,1:T(8,128)(2,1)S(1)} %copy-done.20, bf16[1024,3072]{1,0:T(8,128)(2,1)} %get-tuple-element.308), kind=kOutput, calls=%fused_computation.143 | convolution fusion | flops 4831838208 | bytes 17301504 | tf_op jit(solution)/shard_map/dot_general | solution.py:32
  461.2 12.6 %reshape.265 = f32[768,4,768]{2,1,0:T(4,128)} reshape(f32[768,3072]{1,0:T(8,128)} %fusion.83) | data formatting | bytes 18874368 | tf_op jit(solution)/shard_map/reshape | solution.py:204
  473.7 9.3 copy.204
  486.0 10.0 %convolution_add_fusion.1 = f32[1024,768]{0,1:T(8,128)} fusion(f32[1024,768]{0,1:T(8,128)} %get-tuple-element.293, bf16[1024,2304]{0,1:T(8,128)(2,1)} %copy-done.21, bf16[768,2304]{0,1:T(8,128)(2,1)} %bitcast.218), kind=kOutput, calls=%fused_computation.101 | convolution fusion | flops 3624665088 | bytes 14548992 | tf_op jit(solution)/shard_map/dot_general | solution.py:38
  496.0 3.5 copy.208
  503.4 41.7 %reduce-scatter.15.cloned.1.call-done = f32[96,192]{1,0:T(8,128)} async-done(((f32[3072,192]{1,0:T(8,128)}), f32[96,192]{1,0:T(8,128)}) %reduce-scatter.15.cloned.1.call-update) | async-done | bytes 73744
  546.7 126.2 %reduce-scatter.13.cloned.1.call-done = f32[96,576]{1,0:T(8,128)} async-done(((f32[3072,576]{1,0:T(8,128)}), f32[96,576]{1,0:T(8,128)}) %reduce-scatter.13.cloned.1.call-update) | async-done | bytes 221200
  674.8 139.8 %reduce-scatter.9.cloned.1.call-done = f32[96,768]{1,0:T(8,128)} async-done(((f32[3072,768]{1,0:T(8,128)}), f32[96,768]{1,0:T(8,128)}) %reduce-scatter.9.cloned.1.call-update) | async-done | bytes 294928 | tf_op jit(solution)/shard_map/reduce_scatter | solution.py:205
  814.5 141.6 %reduce-scatter.11.cloned.1.call-done = f32[96,768]{1,0:T(8,128)} async-done(((f32[3072,768]{1,0:T(8,128)}), f32[96,768]{1,0:T(8,128)}) %reduce-scatter.11.cloned.1.call-update) | async-done | bytes 294928 | tf_op jit(solution)/shard_map/reduce_scatter | solution.py:205
  (237 shorter events, 113.9 us)
Async XLA Ops:
  7.2 7.5 copy-start
  7.2 9.9 %copy-start.37 = (bf16[768]{0:T(1024)(128)(2,1)S(1)}, bf16[768]{0:T(1024)(128)(2,1)}, u32[]{:S(2)}) copy-start(bf16[768]{0:T(1024)(128)(2,1)} %param.34) | copy-start | bytes 4612
  7.2 26.3 %copy-start.38 = (bf16[768]{0:T(1024)(128)(2,1)S(1)}, bf16[768]{0:T(1024)(128)(2,1)}, u32[]{:S(2)}) copy-start(bf16[768]{0:T(1024)(128)(2,1)} %param.31) | copy-start | bytes 4612
  7.2 26.9 %copy-start.39 = (bf16[768]{0:T(1024)(128)(2,1)S(1)}, bf16[768]{0:T(1024)(128)(2,1)}, u32[]{:S(2)}) copy-start(bf16[768]{0:T(1024)(128)(2,1)} %param.32) | copy-start | bytes 4612
  7.2 27.5 %copy-start.40 = (bf16[768]{0:T(1024)(128)(2,1)S(1)}, bf16[768]{0:T(1024)(128)(2,1)}, u32[]{:S(2)}) copy-start(bf16[768]{0:T(1024)(128)(2,1)} %param.37) | copy-start | bytes 4612
  7.2 32.7 %copy-start.18 = (bf16[1024,768]{1,0:T(8,128)(2,1)S(1)}, bf16[1024,768]{1,0:T(8,128)(2,1)}, u32[]{:S(2)}) copy-start(bf16[1024,768]{1,0:T(8,128)(2,1)} %param.39) | copy-start | bytes 4718596
  7.2 69.6 %all-gather.8.cloned.1.call-start = ((), (), s32[]{:S(2)}) async-start(), calls=%async_computation.4 | async-start | bytes 4055040 | tf_op jit(solution)/shard_map/all_gather | solution.py:123
  13.2 141.2 %all-gather.10.cloned.1.call-start = ((), (), s32[]{:S(2)}) async-start(), calls=%async_computation.5 | async-start | bytes 1216512 | tf_op jit(solution)/shard_map/all_gather | solution.py:123
  14.6 184.6 %all-gather.12.cloned.1.call-start = ((), (), s32[]{:S(2)}) async-start(), calls=%async_computation.6 | async-start | bytes 4866048 | tf_op jit(solution)/shard_map/all_gather | solution.py:123
  15.4 249.1 %all-gather.14.cloned.1.call-start = ((), (), s32[]{:S(2)}) async-start(), calls=%async_computation.7 | async-start | bytes 4866048 | tf_op jit(solution)/shard_map/all_gather | solution.py:123
  17.1 482.5 %all-gather.16.cloned.1.call-start = ((), (), s32[]{:S(2)}) async-start(), calls=%async_computation.10 | async-start | bytes 1622016 | tf_op jit(solution)/shard_map/all_gather | solution.py:230
  43.0 50.1 %copy-start.14 = (bf16[1024,768]{1,0:T(8,128)(2,1)}, bf16[1024,768]{1,0:T(8,128)(2,1)S(1)}, u32[]{:S(2)}) copy-start(bf16[1024,768]{1,0:T(8,128)(2,1)S(1)} %constant_dynamic-slice_fusion.9) | copy-start | bytes 4718596
  93.1 3.9 copy-start.17
  149.7 4.6 copy-start.36
  158.2 1.7 copy-start.9
  158.3 146.5 %copy-start.24 = (f32[1024]{0:T(1024)}, f32[1024]{0:T(1024)S(1)}, u32[]{:S(2)}) copy-start(f32[1024]{0:T(1024)S(1)} %broadcast_multiply_fusion.5) | copy-start | bytes 12292
  160.3 144.4 %copy-start.29 = (f32[1024]{0:T(1024)}, f32[1024]{0:T(1024)S(1)}, u32[]{:S(2)}) copy-start(f32[1024]{0:T(1024)S(1)} %add_rsqrt_fusion.1) | copy-start | bytes 12292
  199.2 6.7 copy-start.27
  199.2 6.7 copy-start.32
  199.2 6.7 copy-start.33
  205.9 58.5 %copy-start.35 = (f32[768]{0:T(1024)S(1)}, f32[768]{0:T(1024)}, u32[]{:S(2)}) copy-start(f32[768]{0:T(1024)} %convert_element_type.111) | copy-start | bytes 9220
  274.3 2.4 copy-start.31
  275.3 4.0 copy-start.41
  276.7 17.4 %slice-start = ((s8[4718592]{0:T(1024)(128)(4,1)}), s8[4194304]{0:T(1024)(128)(4,1)S(1)}, s32[]{:S(2)}) async-start(s8[4718592]{0:T(1024)(128)(4,1)} %bitcast.214), calls=%async_computation.13 | async-start | bytes 8388608
  279.4 14.7 %copy-start.19 = (bf16[1024,768]{0,1:T(8,128)(2,1)}, bf16[1024,768]{0,1:T(8,128)(2,1)S(1)}, u32[]{:S(2)}) copy-start(bf16[1024,768]{0,1:T(8,128)(2,1)S(1)} %get-tuple-element.291) | copy-start | bytes 4718596
  279.4 14.7 %copy-start.10 = (f32[1024,768]{0,1:T(8,128)S(1)}, f32[1024,768]{0,1:T(8,128)}, u32[]{:S(2)}) copy-start(f32[1024,768]{0,1:T(8,128)} %copy-done.9) | copy-start | bytes 9437188
  279.4 14.7 %slice-start.1 = ((s8[4718592]{0:T(1024)(128)(4,1)}), s8[524288]{0:T(1024)(128)(4,1)S(1)}, s32[]{:S(2)}) async-start(s8[4718592]{0:T(1024)(128)(4,1)} %bitcast.214), calls=%async_computation.14 | async-start | bytes 1048576
  329.7 3.1 copy-start.4
  332.8 4.0 copy-start.3
  343.6 7.1 copy-start.11
  350.7 2.0 copy-start.2
  350.7 2.0 copy-start.5
  355.4 3.1 copy-start.4
  358.5 4.0 copy-start.3
  369.4 7.1 copy-start.11
  376.5 2.0 copy-start.2
  376.5 2.0 copy-start.5
  380.9 3.6 copy-start.22
  380.9 3.6 copy-start.23
  385.2 159.9 %reduce-scatter.15.cloned.1.call-start = ((), (), s32[]{:S(2)}) async-start(), calls=%async_computation.12 | async-start | bytes 3244032
  391.4 3.7 copy-start.7
  391.4 281.5 %reduce-scatter.13.cloned.1.call-start = ((), (), s32[]{:S(2)}) async-start(), calls=%async_computation.11 | async-start | bytes 8110080
  391.9 4.8 copy-start.13
  401.1 3.9 copy-start.21
  416.7 397.9 %reduce-scatter.9.cloned.1.call-start = ((), (), s32[]{:S(2)}) async-start(), calls=%async_computation.8 | async-start | bytes 9732096 | tf_op jit(solution)/shard_map/reduce_scatter | solution.py:205
  449.5 1.4 copy-start.20
  449.5 506.7 %reduce-scatter.11.cloned.1.call-start = ((), (), s32[]{:S(2)}) async-start(), calls=%async_computation.9 | async-start | bytes 9732096 | tf_op jit(solution)/shard_map/reduce_scatter | solution.py:205
  486.0 470.2 %copy-start.1 = (bf16[768,768]{1,0:T(8,128)(2,1)S(1)}, bf16[768,768]{1,0:T(8,128)(2,1)}, u32[]{:S(2)}) copy-start(bf16[768,768]{1,0:T(8,128)(2,1)} %param.33) | copy-start | bytes 3538948
  (12 other events, 13.2 us)
Sparse Core Ops, SparseCore 0:
  13.3 63.5 all-gather.7
  80.4 52.7 all-gather.9
  136.6 62.4 all-gather.11
  202.5 61.9 all-gather.13
  385.4 53.2 all-gather.15
  444.0 101.0 reduce-scatter.14
  550.8 122.1 reduce-scatter.12
  679.4 135.0 reduce-scatter.8
  821.0 135.1 reduce-scatter.10
